TPU v7x, 128 devices: a whole 4x4x4 slice. The times are simulated.
128 devices in a mesh: tile: 16 (over x_lo, z, core), chan: 8 (over y, x_hi).
Axes of the slice: x: 4 (x_hi: 2, x_lo: 2; x = x_hi * 2 + x_lo), y: 4, z: 4, core: 2. Of those that a mesh axis runs over, the one named last changes fastest.
Arguments:
- voltages: int32 [512, 262144], P('tile', 'chan'), may hold values from -128 to 127
- history: int32 [512, 30720], P('tile'), may hold values from -128 to 127
- filter_taps: int32 [16, 2048], replicated, may hold values from -64 to 64
Outputs:
- visibilities: float32 [2, 1024, 512, 512], P(None, 'chan', 'tile')
Inputs may be any that keep to these rules, and one draw needn't show every extreme that they name: `voltages`: 8-bit signed samples. `history`: 8-bit signed samples.
All inputs are finite; a program needn't handle non-finite values.
Results may differ from a plain program's by a relative error of at most 0.006.
Values may be sent and summed in bfloat16 or wider, within the bound.
A program may use at most 192 MiB of HBM per device.

v0:
```python
import math
import jax
import jax.numpy as jnp
from jax import lax
from jax.sharding import PartitionSpec as P

CH = 1024
TAPS = 16
FFT = 2048
filter_norm = 1.0 / 16384.0


def from_behind(value, axis, steps):
    count = lax.axis_size(axis)
    leading, last = (max(0, -steps), min(count, count - steps))
    return lax.ppermute(value, axis, [(source, source + steps) for source in range(leading, last)])


def dft_table(samples, channels):
    rows_index = jnp.arange(samples, dtype=jnp.int32)[:, None]
    cols_index = jnp.arange(channels, dtype=jnp.int32)[None, :]
    angles = (rows_index * cols_index % samples).astype(jnp.float32) * (2.0 * math.pi / samples)
    factor = 1.0 / math.sqrt(channels)
    return jnp.concatenate([jnp.cos(angles) * factor, -jnp.sin(angles) * factor], axis=1).astype(
        jnp.bfloat16
    )


def polyphase(extended, weights, spectra_count):
    summed = jnp.zeros((extended.shape[0], spectra_count, extended.shape[2]), jnp.float32)
    for tap_index in range(weights.shape[0]):
        summed = (
            summed
            + weights[tap_index][None, None, :]
            * extended[:, tap_index : tap_index + spectra_count, :]
        )
    return summed


def counter_rows(spectra):
    real_part = spectra[:, :, 0]
    imag_part = spectra[:, :, 1]
    rotated = jnp.stack([imag_part, -real_part], axis=2)
    return jnp.stack([spectra, rotated], axis=0)


def body(voltages, history, filter_taps):
    local_inputs = voltages.shape[0]
    spectra_count = voltages.shape[1] // FFT
    tail_blocks = voltages[:, (spectra_count - TAPS + 1) * FFT :].astype(jnp.bfloat16)
    carried = from_behind(tail_blocks, "chan", 1)
    is_first = lax.axis_index("chan") == 0
    earlier = jnp.where(is_first, history.astype(jnp.float32), carried.astype(jnp.float32))
    extended = jnp.concatenate([earlier, voltages.astype(jnp.float32)], axis=1)
    extended = extended.reshape(local_inputs, spectra_count + TAPS - 1, FFT)
    filtered = (
        polyphase(extended, filter_taps.astype(jnp.float32), spectra_count) * filter_norm
    ).astype(jnp.bfloat16)
    spectra = jnp.dot(
        filtered.reshape(-1, FFT), dft_table(FFT, CH), preferred_element_type=jnp.float32
    )
    spectra = spectra.reshape(local_inputs, spectra_count, 2, CH).astype(jnp.bfloat16)
    turned = lax.all_to_all(spectra, "chan", split_axis=3, concat_axis=1, tiled=True)
    total_spectra = turned.shape[1]
    average = 1.0 / total_spectra
    row_sets = counter_rows(turned)
    return (
        jnp.einsum(
            "qaspc,bspc->qcab",
            row_sets,
            lax.all_gather(turned, "tile", axis=0, tiled=True),
            preferred_element_type=jnp.float32,
        )
        * average
    )


def solution(mesh):
    in_specs = (P("tile", "chan"), P("tile", None), P())
    out_specs = P(None, "chan", "tile", None)
    return jax.shard_map(body, mesh=mesh, in_specs=in_specs, out_specs=out_specs, check_vma=False)
```

profile of v0, /device:TPU:1, one launch (start us, length us, event | category | flops | bytes accessed | tf_op | source)
XLA Modules:
  0.0 409.3 jit_solution(11984337973401259222)
XLA Ops:
  6.5 0.0 copy-start.3
  6.5 0.0 all-gather.2.cloned.1.call-start
  6.5 0.0 copy-start.1
  6.5 3.7 slice_convert_fusion
  10.3 5.6 %collective-permute-start = (bf16[32,30720]{1,0:T(8,128)(2,1)}, bf16[32,30720]{1,0:T(8,128)(2,1)S(1)}, u32[]{:S(2)}, u32[]{:S(2)}) collective-permute-start(bf16[32,30720]{1,0:T(8,128)(2,1)} %slice_convert_fusion), channel_id=1, source_target_pairs={{0,1},{1,2},{2,3},{3,4},{4,5},{5,6},{6,7},{8,9},{9,10},{10,11},{11... | collective-permute-start | bytes 5898248 | tf_op jit(solution)/shard_map/ppermute | solution.py:16
  15.9 0.0 copy-done.3
  15.9 0.1 fusion.40
  16.0 0.0 copy-done.1
  16.0 2.2 convert_element_type.28
  18.2 34.9 %multiply_convert_fusion = (bf16[2048,1024]{0,1:T(8,128)(2,1)}, bf16[2048,1024]{0,1:T(8,128)(2,1)}) fusion(), kind=kLoop, calls=%fused_computation.11 | loop fusion | flops 39845888 | bytes 8388608 | tf_op jit(solution)/shard_map/convert.1
  53.2 8.5 %pad_maximum_fusion = bf16[2048,2048]{0,1:T(8,128)(2,1)} fusion(bf16[2048,1024]{0,1:T(8,128)(2,1)} %get-tuple-element.23, bf16[2048,1024]{0,1:T(8,128)(2,1)} %get-tuple-element.24), kind=kLoop, calls=%fused_computation.10 | loop fusion | flops 16777216 | bytes 16777216 | tf_op jit(solution)/shard_map/concatenate | solution.py:24
  61.7 0.0 copy-start
  61.7 0.0 collective-permute-done
  61.7 2.6 convert_select_fusion
  64.4 0.7 copy-done
  65.1 3.7 pad_maximum_fusion.1
  68.7 7.6 %reshape.25 = f32[32,31,2048]{2,1,0:T(8,128)} reshape(f32[32,63488]{1,0:T(8,128)} %pad_maximum_fusion.1) | data formatting | bytes 16252928 | tf_op jit(solution)/shard_map/reshape | solution.py:55
  76.4 43.5 %fusion.34 = bf16[32,16,2,1024]{3,1,2,0:T(8,128)(2,1)S(1)} fusion(bf16[2,1024,2048,1]{2,1,0,3:T(8,128)(2,1)} %bitcast.59, f32[32,31,2048]{2,1,0:T(8,128)} %reshape.25, f32[2048]{0:T(1024)S(1)} %bitcast.61, f32[2048]{0:T(1024)S(1)} %bitcast.62, f32[2048]{0:T(1024)S(1)} %bitcast.63, f32[2048]{0:T(1024)S(1)} %bitcast.64, f32[2048]{0:T(1024)S(1)} %bitcast.65, ...), kind=kOutput, calls=%fused_computation.58 | convolution fusion | flops 4330618880 | bytes 77725696 | tf_op jit(solution)/shard_map/dot_general | solution.py:59
  119.9 12.8 %copy.28 = bf16[32,16,2,1024]{0,1,2,3:T(8,128)(2,1)} copy(bf16[32,16,2,1024]{3,1,2,0:T(8,128)(2,1)S(1)} %fusion.34) | data formatting | bytes 4194304 | tf_op jit(solution)/shard_map/convert_element_type | solution.py:62
  132.7 10.1 %reshape.30 = bf16[8,2,65536]{2,1,0:T(2,128)(2,1)S(1)} reshape(bf16[1024,2,16,32]{3,2,1,0:T(8,128)(2,1)} %bitcast.55) | data formatting | bytes 4194304
  142.9 31.9 %all_to_all.18 = bf16[8,2,65536]{2,1,0:T(2,128)(2,1)} all-to-all(bf16[8,2,65536]{2,1,0:T(2,128)(2,1)S(1)} %reshape.30), channel_id=1, replica_groups=mesh['tile'=16,'chan'=8] {'chan'}, dimensions={0} | all-to-all | bytes 4194304 | tf_op jit(solution)/shard_map/all_to_all | solution.py:63
  174.8 8.6 %reshape.31 = bf16[1024,2,16,32]{3,2,1,0:T(8,128)(2,1)} reshape(bf16[8,2,65536]{2,1,0:T(2,128)(2,1)} %all_to_all.18) | data formatting | bytes 4194304
  183.4 10.3 %copy.30 = bf16[32,8,16,2,128]{4,2,1,3,0:T(8,128)(2,1)S(1)} copy(bf16[32,8,16,2,128]{0,2,3,4,1:T(8,128)(2,1)} %bitcast.56) | data formatting | bytes 4194304 | tf_op jit(solution)/shard_map/all_to_all | solution.py:63
  193.7 2.9 copy.31
  196.6 0.0 all-gather.2.cloned.1.call-update
  196.6 3.0 copy.35
  199.6 0.0 copy-start.2
  199.6 1.9 fusion.39
  201.5 1.5 maximum_bitcast_fusion
  203.1 165.1 %all-gather.2.cloned.1.call-done = bf16[512,128,2,128]{1,0,2,3:T(8,128)(2,1)} async-done(((bf16[32,128,2,128]{1,0,2,3:T(8,128)(2,1)}), bf16[512,128,2,128]{1,0,2,3:T(8,128)(2,1)}) %all-gather.2.cloned.1.call-update) | async-done | bytes 33554448 | tf_op jit(solution)/shard_map/all_gather | solution.py:71
  368.1 0.0 copy-done.2
  368.1 21.9 %fusion.2 = f32[2,128,32,512]{3,2,0,1:T(8,128)} fusion(bf16[512,128,2,128]{1,0,2,3:T(8,128)(2,1)} %all-gather.2.cloned.1.call-done, bf16[1,32,128,2,128]{2,1,3,0,4:T(8,128)(2,1)} %maximum_bitcast_fusion, bf16[1,32,128,2,128]{2,1,3,0,4:T(8,128)(2,1)S(1)} %copy-done.2), kind=kOutput, calls=%fused_computation.3 | convolution fusion | flops 2160066560 | bytes 54525952 | tf_op jit(solution)/shard_map/qaspc,bspc->qcab/dot_general | solution.py:68
  390.1 12.4 %copy.36 = f32[2,128,32,512]{3,2,1,0:T(8,128)} copy(f32[2,128,32,512]{3,2,0,1:T(8,128)} %fusion.2) | data formatting | bytes 33554432 | tf_op jit(solution)/shard_map/mul | solution.py:68
  (1 shorter events, 0.0 us)
Async XLA Ops:
  6.5 9.3 %copy-start.3 = (s32[16,2048]{1,0:T(8,128)S(1)}, s32[16,2048]{1,0:T(8,128)}, u32[]{:S(2)}) copy-start(s32[16,2048]{1,0:T(8,128)} %param.5) | copy-start | bytes 393220
  6.5 361.6 %all-gather.2.cloned.1.call-start = ((), (), s32[]{:S(2)}) async-start(), calls=%async_computation.1 | async-start | bytes 35651584 | tf_op jit(solution)/shard_map/all_gather | solution.py:71
  6.5 9.5 %copy-start.1 = (s32[32,32768]{1,0:T(8,128)S(1)}, s32[32,32768]{1,0:T(8,128)}, u32[]{:S(2)}) copy-start(s32[32,32768]{1,0:T(8,128)} %param.3) | copy-start | bytes 12582916
  10.3 51.4 %collective-permute-start = (bf16[32,30720]{1,0:T(8,128)(2,1)}, bf16[32,30720]{1,0:T(8,128)(2,1)S(1)}, u32[]{:S(2)}, u32[]{:S(2)}) collective-permute-start(bf16[32,30720]{1,0:T(8,128)(2,1)} %slice_convert_fusion), channel_id=1, source_target_pairs={{0,1},{1,2},{2,3},{3,4},{4,5},{5,6},{6,7},{8,9},{9,10},{10,11},{11... | collective-permute-start | bytes 5898248 | tf_op jit(solution)/shard_map/ppermute | solution.py:16
  61.7 3.4 copy-start
  199.6 168.5 %copy-start.2 = (bf16[1,32,128,2,128]{2,1,3,0,4:T(8,128)(2,1)S(1)}, bf16[1,32,128,2,128]{2,1,3,0,4:T(8,128)(2,1)}, u32[]{:S(2)}) copy-start(bf16[1,32,128,2,128]{2,1,3,0,4:T(8,128)(2,1)} %copy.35) | copy-start | bytes 6291460
Sparse Core Ops, SparseCore 0:
  196.8 171.3 all-gather.1
where the time goes:
time: 410 us; the launch traced here: 409 us
  waiting for transfers between devices  165 us (40%)
  local copies, waits for them, and re-layouts  68.6 us (17%)
  matrix products  65.5 us (16%)
  other arithmetic  59.2 us (14%)
  blocking collectives  31.9 us (8%)
  between operations  13.5 us (3%)
  starting transfers between devices  5.58 us (1%)
    all_gather x1, waiting for transfers between devices, body(): lax.all_gather(turned, 'tile', axis=0, tiled=True)  165 us
    dot_general x1, matrix products, body(): jnp.dot(filtered.reshape(-1, FFT), dft_table(FFT, CH), preferred_element_...  43.5 us
    another operation x2, other arithmetic  38.7 us
    all_to_all x1, blocking collectives, body(): lax.all_to_all(spectra, 'chan', split_axis=3, concat_axis=1, tiled=True)  31.9 us
    dot_general x1, matrix products, body(): jnp.einsum('qaspc,bspc->qcab', row_sets, lax.all_gather(turned, 'tile', a...  21.9 us
    unnamed x10, local copies, waits for them, and re-layouts  19.5 us
    all_to_all x2, local copies, waits for them, and re-layouts, body(): lax.all_to_all(spectra, 'chan', split_axis=3, concat_axis=1, tiled=True)  13.2 us
    convert_element_type x1, local copies, waits for them, and re-layouts, body(): spectra.reshape(local_inputs, spectra_count, 2, CH).astype(jnp.bfloat16)  12.8 us
  transfers between devices with their start and end apart: 2, of which 1 were waited for; matrix products, arithmetic and copies ran while one was open for 13% of the time, Pallas kernels for 0%

commit v1 on v0

--- a/solution.py
+++ b/solution.py
@@ -60,7 +60,16 @@
         filtered.reshape(-1, FFT), dft_table(FFT, CH), preferred_element_type=jnp.float32
     )
     spectra = spectra.reshape(local_inputs, spectra_count, 2, CH).astype(jnp.bfloat16)
-    turned = lax.all_to_all(spectra, "chan", split_axis=3, concat_axis=1, tiled=True)
+    press_indices = lambda chunk: jnp.concatenate(
+        jax.lax.all_to_all(
+            jnp.stack(jnp.split(chunk, jax.lax.axis_size("chan"), 3)),
+            axis_name="chan",
+            split_axis=0,
+            concat_axis=0,
+        ),
+        axis=1,
+    )
+    turned = press_indices(spectra)
     total_spectra = turned.shape[1]
     average = 1.0 / total_spectra
     row_sets = counter_rows(turned)

time: 410 us -> 370 us (0.902)
  local copies, waits for them, and re-layouts: 68.6 us -> 31.1 us
    unnamed x10 -> x19, local copies, waits for them, and re-layouts: 19.5 us -> 2.68 us
    all_to_all x2 -> x0, local copies, waits for them, and re-layouts: 13.2 us -> none  [body(): lax.all_to_all(spectra, 'chan', split_axis=3, concat_axis=1, tiled=True)]
    convert_element_type x1 -> x0, local copies, waits for them, and re-layouts: 12.8 us -> none  [body(): spectra.reshape(local_inputs, spectra_count, 2, CH).astype(jnp.bfloat16)]
  transfers between devices with their start and end apart: 2 -> 2, of which waited for: 1 -> 1; matrix products, arithmetic and copies ran while one was open for 13% -> 14% of each run, Pallas kernels for 0% -> 0%
where the time goes in v1:
time: 370 us
  waiting for transfers between devices  165 us (45%)
  matrix products  65 us (18%)
  other arithmetic  57.5 us (16%)
  blocking collectives  31.8 us (9%)
  local copies, waits for them, and re-layouts  31.1 us (8%)
  between operations  13.5 us (4%)
  starting transfers between devices  5.58 us (2%)
    all_gather x1, waiting for transfers between devices, body(): lax.all_gather(turned, 'tile', axis=0, tiled=True)  165 us
    dot_general x1, matrix products, body(): jnp.dot(filtered.reshape(-1, FFT), dft_table(FFT, CH), preferred_element_...  43.1 us
    another operation x2, other arithmetic  38.7 us
    all_to_all x1, blocking collectives, body(): jax.lax.all_to_all(jnp.stack(jnp.split(chunk, jax.lax.axis_size('chan'),...  31.8 us
    dot_general x1, matrix products, body(): jnp.einsum('qaspc,bspc->qcab', row_sets, lax.all_gather(turned, 'tile', a...  22 us
    mul x1, local copies, waits for them, and re-layouts, body(): jnp.einsum('qaspc,bspc->qcab', row_sets, lax.all_gather(turned, 'tile', a...  12.4 us
    concatenate x1, other arithmetic, dft_table(): jnp.concatenate([jnp.cos(angles) * factor, -jnp.sin(angles) * factor], ax...  8.53 us
    reshape x1, local copies, waits for them, and re-layouts, body(): extended = extended.reshape(local_inputs, spectra_count + TAPS - 1, FFT)  7.63 us
  transfers between devices with their start and end apart: 2, of which 1 were waited for; matrix products, arithmetic and copies ran while one was open for 14% of the time, Pallas kernels for 0%

profile of v1, /device:TPU:1, one launch (start us, length us, event | category | flops | bytes accessed | tf_op | source)
XLA Modules:
  0.0 369.6 jit_solution(14210460006169016203)
XLA Ops:
  6.5 0.0 copy-start.5
  6.5 0.0 all-gather.2.cloned.1.call-start
  6.5 0.0 copy-start.3
  6.5 3.8 %slice_convert_fusion = bf16[32,30720]{1,0:T(8,128)(2,1)} fusion(s32[32,32768]{1,0:T(8,128)} %param.3), kind=kLoop, calls=%fused_computation.53 | loop fusion | flops 983040 | bytes 5898240 | tf_op jit(solution)/shard_map/convert.2
  10.3 5.6 %collective-permute-start = (bf16[32,30720]{1,0:T(8,128)(2,1)}, bf16[32,30720]{1,0:T(8,128)(2,1)S(1)}, u32[]{:S(2)}, u32[]{:S(2)}) collective-permute-start(bf16[32,30720]{1,0:T(8,128)(2,1)} %slice_convert_fusion), channel_id=1, source_target_pairs={{0,1},{1,2},{2,3},{3,4},{4,5},{5,6},{6,7},{8,9},{9,10},{10,11},{11... | collective-permute-start | bytes 5898248 | tf_op jit(solution)/shard_map/ppermute | solution.py:16
  15.9 0.0 copy-done.5
  15.9 0.1 fusion.48
  16.0 0.0 copy-done.3
  16.0 2.2 convert_element_type.28
  18.2 34.9 %multiply_convert_fusion = (bf16[2048,1024]{0,1:T(8,128)(2,1)}, bf16[2048,1024]{0,1:T(8,128)(2,1)}) fusion(), kind=kLoop, calls=%fused_computation.11 | loop fusion | flops 39845888 | bytes 8388608 | tf_op jit(solution)/shard_map/convert.1
  53.2 8.5 %pad_maximum_fusion = bf16[2048,2048]{0,1:T(8,128)(2,1)} fusion(bf16[2048,1024]{0,1:T(8,128)(2,1)} %get-tuple-element.23, bf16[2048,1024]{0,1:T(8,128)(2,1)} %get-tuple-element.24), kind=kLoop, calls=%fused_computation.10 | loop fusion | flops 16777216 | bytes 16777216 | tf_op jit(solution)/shard_map/concatenate | solution.py:24
  61.7 0.0 copy-start.2
  61.7 0.0 collective-permute-done
  61.7 2.6 convert_select_fusion
  64.4 0.7 copy-done.2
  65.1 3.7 pad_maximum_fusion.1
  68.7 7.6 %reshape.30 = f32[32,31,2048]{2,1,0:T(8,128)} reshape(f32[32,63488]{1,0:T(8,128)} %pad_maximum_fusion.1) | data formatting | bytes 16252928 | tf_op jit(solution)/shard_map/reshape | solution.py:55
  76.4 43.1 %fusion.34 = bf16[32,16,2,1024]{3,1,2,0:T(8,128)(2,1)S(1)} fusion(bf16[2,1024,2048,1]{2,1,0,3:T(8,128)(2,1)} %bitcast.82, f32[32,31,2048]{2,1,0:T(8,128)} %reshape.30, f32[2048]{0:T(1024)S(1)} %bitcast.85, f32[2048]{0:T(1024)S(1)} %bitcast.86, f32[2048]{0:T(1024)S(1)} %bitcast.87, f32[2048]{0:T(1024)S(1)} %bitcast.88, f32[2048]{0:T(1024)S(1)} %bitcast.89, ...), kind=kOutput, calls=%fused_computation.58 | convolution fusion | flops 4330618880 | bytes 77725696 | tf_op jit(solution)/shard_map/dot_general | solution.py:59
  119.4 0.1 fusion.44
  119.5 0.1 fusion.43
  119.6 0.1 fusion.42
  119.7 0.1 fusion.41
  119.8 0.1 fusion.40
  119.9 0.1 fusion.39
  120.0 0.1 fusion.38
  120.1 0.1 fusion.37
  120.2 31.8 %all_to_all.5 = bf16[8,32,16,2,128]{4,2,3,1,0:T(8,128)(2,1)S(1)} all-to-all(bf16[8,32,16,2,128]{4,2,3,1,0:T(8,128)(2,1)S(1)} %fusion.37), channel_id=1, replica_groups=mesh['tile'=16,'chan'=8] {'chan'}, dimensions={0} | all-to-all | bytes 4194304 | tf_op jit(solution)/shard_map/all_to_all | solution.py:64
  152.0 0.6 copy.5
  152.6 0.0 copy-start.1
  152.7 1.3 copy-done.1
  154.0 2.9 copy.6
  156.9 0.0 copy-start
  156.9 0.0 all-gather.2.cloned.1.call-update
  156.9 4.8 %copy.10 = bf16[1,32,128,2,128]{2,1,3,0,4:T(8,128)(2,1)} copy(bf16[1,32,128,2,128]{4,2,3,1,0:T(8,128)(2,1)} %bitcast.81) | data formatting | bytes 4194304 | tf_op jit(solution)/shard_map/stack;reshape | solution.py:44
  161.7 0.0 copy-done
  161.7 0.2 fusion.47
  161.9 0.0 copy-start.4
  161.9 1.5 maximum_bitcast_fusion
  163.4 165.0 %all-gather.2.cloned.1.call-done = bf16[512,128,2,128]{1,0,2,3:T(8,128)(2,1)} async-done(((bf16[32,128,2,128]{1,0,2,3:T(8,128)(2,1)}), bf16[512,128,2,128]{1,0,2,3:T(8,128)(2,1)}) %all-gather.2.cloned.1.call-update) | async-done | bytes 33554448 | tf_op jit(solution)/shard_map/all_gather | solution.py:80
  328.4 0.0 copy-done.4
  328.4 22.0 %fusion.2 = f32[2,128,32,512]{3,2,0,1:T(8,128)} fusion(bf16[512,128,2,128]{1,0,2,3:T(8,128)(2,1)} %all-gather.2.cloned.1.call-done, bf16[1,32,128,2,128]{2,1,3,0,4:T(8,128)(2,1)} %maximum_bitcast_fusion, bf16[1,32,128,2,128]{2,1,3,0,4:T(8,128)(2,1)S(1)} %copy-done.4), kind=kOutput, calls=%fused_computation.3 | convolution fusion | flops 2160066560 | bytes 54525952 | tf_op jit(solution)/shard_map/qaspc,bspc->qcab/dot_general | solution.py:77
  350.3 12.4 %copy.11 = f32[2,128,32,512]{3,2,1,0:T(8,128)} copy(f32[2,128,32,512]{3,2,0,1:T(8,128)} %fusion.2) | data formatting | bytes 33554432 | tf_op jit(solution)/shard_map/mul | solution.py:77
  (1 shorter events, 0.0 us)
Async XLA Ops:
  6.5 9.3 %copy-start.5 = (s32[16,2048]{1,0:T(8,128)S(1)}, s32[16,2048]{1,0:T(8,128)}, u32[]{:S(2)}) copy-start(s32[16,2048]{1,0:T(8,128)} %param.5) | copy-start | bytes 393220
  6.5 321.8 %all-gather.2.cloned.1.call-start = ((), (), s32[]{:S(2)}) async-start(), calls=%async_computation.1 | async-start | bytes 35651584 | tf_op jit(solution)/shard_map/all_gather | solution.py:80
  6.5 9.5 %copy-start.3 = (s32[32,32768]{1,0:T(8,128)S(1)}, s32[32,32768]{1,0:T(8,128)}, u32[]{:S(2)}) copy-start(s32[32,32768]{1,0:T(8,128)} %param.3) | copy-start | bytes 12582916
  10.3 51.4 %collective-permute-start = (bf16[32,30720]{1,0:T(8,128)(2,1)}, bf16[32,30720]{1,0:T(8,128)(2,1)S(1)}, u32[]{:S(2)}, u32[]{:S(2)}) collective-permute-start(bf16[32,30720]{1,0:T(8,128)(2,1)} %slice_convert_fusion), channel_id=1, source_target_pairs={{0,1},{1,2},{2,3},{3,4},{4,5},{5,6},{6,7},{8,9},{9,10},{10,11},{11... | collective-permute-start | bytes 5898248 | tf_op jit(solution)/shard_map/ppermute | solution.py:16
  61.7 3.4 copy-start.2
  152.6 1.3 copy-start.1
  156.9 4.8 %copy-start = (bf16[32,128,2,128]{1,0,2,3:T(8,128)(2,1)S(1)}, bf16[32,128,2,128]{1,0,2,3:T(8,128)(2,1)}, u32[]{:S(2)}) copy-start(bf16[32,128,2,128]{1,0,2,3:T(8,128)(2,1)} %copy.6) | copy-start | bytes 6291460
  161.9 166.5 %copy-start.4 = (bf16[1,32,128,2,128]{2,1,3,0,4:T(8,128)(2,1)S(1)}, bf16[1,32,128,2,128]{2,1,3,0,4:T(8,128)(2,1)}, u32[]{:S(2)}) copy-start(bf16[1,32,128,2,128]{2,1,3,0,4:T(8,128)(2,1)} %copy.10) | copy-start | bytes 6291460
Sparse Core Ops, SparseCore 0:
  157.0 171.3 all-gather.1
